TPU v7x, 256 devices: a whole 4x4x8 slice. The times are simulated.
256 devices in a mesh: ctx: 32 (over z, y_lo, core), head: 8 (over x, y_hi).
Axes of the slice: x: 4, y: 4 (y_hi: 2, y_lo: 2; y = y_hi * 2 + y_lo), z: 8, core: 2. Of those that a mesh axis runs over, the one named last changes fastest.
Arguments:
- queries: bfloat16 [4096, 8192], P('ctx', 'head'), may hold values from -5 to 5
- key_rows: bfloat16 [4096, 1024], P('ctx', 'head'), may hold values from -5 to 5
- value_rows: bfloat16 [4096, 1024], P('ctx', 'head'), may hold values from -6 to 6
- query_tangent: bfloat16 [4096, 8192], P('ctx', 'head'), may hold values from -16 to 16
- key_tangent: bfloat16 [4096, 1024], P('ctx', 'head'), may hold values from -3 to 3
- value_tangent: bfloat16 [4096, 1024], P('ctx', 'head'), may hold values from -6 to 6
- block_order: int32 [32], replicated, may hold values from 0 to 31, each once
Outputs:
- attended: bfloat16 [4096, 8192], P('ctx', 'head')
- probe_out: bfloat16 [4096, 8192], P('ctx', 'head')
- probe_norm: float32 [], replicated
Inputs may be any that keep to these rules, and one draw needn't show every extreme that they name: `block_order`: each block index appears exactly once.
All inputs are finite; a program needn't handle non-finite values.
Results may differ from a plain program's by a relative error of at most 0.025.
Values may be sent and summed in bfloat16 or wider, within the bound.
No kernel may reach another device: no remote copies, remote signals or barrier semaphores. Data moves between devices by JAX's collectives and lax.ppermute only.
A program may use at most 64 MiB of HBM per device.

v0:
```python
import math
import jax
import jax.numpy as jnp
from jax import lax
from jax.sharding import PartitionSpec as P

HEAD_DIM = 128
floor_score = -1e30


def lookup(table, entries):
    return jnp.sum(jnp.where(entries[..., None] == jnp.arange(table.shape[0]), table, 0), axis=-1)


def attend(
    query_block, qtan_block, key_block, value_block, ktan_block, vtan_block, visible, running
):
    factor = 1.0 / math.sqrt(query_block.shape[-1])
    scores = (
        jnp.einsum("tghd,sgd->tghs", query_block, key_block, preferred_element_type=jnp.float32)
        * factor
    )
    scores = jnp.where(visible[:, None, None, :], scores, floor_score)
    top_old, totals_old, drifts_old, numer_old, tangent_old = running
    top_new = jnp.maximum(top_old, jnp.max(scores, axis=-1))
    shrink = jnp.exp(top_old - top_new)
    weights = jnp.exp(scores - top_new[..., None])
    weights = jnp.where(visible[:, None, None, :], weights, 0.0)
    slopes = (
        jnp.einsum("tghd,sgd->tghs", qtan_block, key_block, preferred_element_type=jnp.float32)
        + jnp.einsum("tghd,sgd->tghs", query_block, ktan_block, preferred_element_type=jnp.float32)
    ) * factor
    tilted = weights * slopes
    totals = shrink * totals_old + jnp.sum(weights, axis=-1)
    drifts = shrink * drifts_old + jnp.sum(tilted, axis=-1)
    low_weights = weights.astype(jnp.bfloat16)
    low_tilted = tilted.astype(jnp.bfloat16)
    numerator = shrink[..., None] * numer_old + jnp.einsum(
        "tghs,sgd->tghd", low_weights, value_block, preferred_element_type=jnp.float32
    )
    tangent_num = (
        shrink[..., None] * tangent_old
        + jnp.einsum("tghs,sgd->tghd", low_tilted, value_block, preferred_element_type=jnp.float32)
        + jnp.einsum("tghs,sgd->tghd", low_weights, vtan_block, preferred_element_type=jnp.float32)
    )
    return (top_new, totals, drifts, numerator, tangent_num)


def empty_sums(q_four):
    stat_shape = q_four.shape[:3]
    return (
        jnp.full(stat_shape, floor_score, jnp.float32),
        jnp.zeros(stat_shape, jnp.float32),
        jnp.zeros(stat_shape, jnp.float32),
        jnp.zeros(q_four.shape, jnp.float32),
        jnp.zeros(q_four.shape, jnp.float32),
    )


def make_fold(q_four, dq_four, query_pos, block_order, block_rows):

    def fold_keys(running, pieces, start):
        length = pieces[0].shape[0]
        span = 512

        def sweep(sweep_no, held):
            offset = sweep_no * span
            k_part = lax.dynamic_slice_in_dim(pieces[0], offset, span, 0)
            v_part = lax.dynamic_slice_in_dim(pieces[1], offset, span, 0)
            dk_part = lax.dynamic_slice_in_dim(pieces[2], offset, span, 0)
            dv_part = lax.dynamic_slice_in_dim(pieces[3], offset, span, 0)
            key_index = offset + jnp.arange(span, dtype=jnp.int32)
            key_pos = (
                lookup(block_order, key_index // block_rows) * block_rows + key_index % block_rows
            )
            visible = key_pos[None, :] <= query_pos[:, None]
            return attend(q_four, dq_four, k_part, v_part, dk_part, dv_part, visible, held)

        return lax.fori_loop(0, length // span, sweep, running)

    return fold_keys


def finish(final, width):
    top_final, totals, drifts, numerator, tangent_num = final
    rows = numerator.shape[0]
    attended = (numerator / totals[..., None]).astype(jnp.bfloat16).reshape(rows, width)
    probe = (tangent_num - numerator * drifts[..., None] / totals[..., None]) / totals[..., None]
    square_sum = jnp.sum(probe * probe)
    probe_out = probe.astype(jnp.bfloat16).reshape(rows, width)
    return (attended, probe_out, square_sum)


def shards(queries, key_rows, value_rows, query_tangent, key_tangent, value_tangent, block_order):
    row_count = queries.shape[0]
    width = queries.shape[1]
    groups = key_rows.shape[1] // HEAD_DIM
    shares = width // key_rows.shape[1]
    q_four = queries.reshape(row_count, groups, shares, HEAD_DIM)
    dq_four = query_tangent.reshape(row_count, groups, shares, HEAD_DIM)
    k_three = key_rows.reshape(row_count, groups, HEAD_DIM)
    v_three = value_rows.reshape(row_count, groups, HEAD_DIM)
    dk_three = key_tangent.reshape(row_count, groups, HEAD_DIM)
    dv_three = value_tangent.reshape(row_count, groups, HEAD_DIM)
    empty = empty_sums(q_four)
    count = lax.axis_size("ctx")
    own_index = lax.axis_index("ctx")
    own_block = lookup(block_order, own_index)
    local_rows = jnp.arange(row_count, dtype=jnp.int32)
    query_pos = own_block * row_count + local_rows
    fold_keys = make_fold(q_four, dq_four, query_pos, block_order, row_count)
    final = fold_keys(
        empty,
        (
            lax.all_gather(k_three, "ctx", axis=0, tiled=True),
            lax.all_gather(v_three, "ctx", axis=0, tiled=True),
            lax.all_gather(dk_three, "ctx", axis=0, tiled=True),
            lax.all_gather(dv_three, "ctx", axis=0, tiled=True),
        ),
        jnp.int32(0),
    )
    attended, probe_out, square_sum = finish(final, width)
    total_squares = lax.psum(square_sum, ("ctx", "head"))
    entries = row_count * width * count * lax.axis_size("head")
    probe_norm = jnp.sqrt(total_squares / entries)
    return (attended, probe_out, probe_norm)


def solution(mesh):
    in_specs = (
        P("ctx", "head"),
        P("ctx", "head"),
        P("ctx", "head"),
        P("ctx", "head"),
        P("ctx", "head"),
        P("ctx", "head"),
        P(),
    )
    out_specs = (P("ctx", "head"), P("ctx", "head"), P())
    return jax.shard_map(shards, mesh=mesh, in_specs=in_specs, out_specs=out_specs, check_vma=False)
```

profile of v0, /device:TPU:1, one launch (start us, length us, event | category | flops | bytes accessed | tf_op | source)
XLA Modules:
  0.0 435.9 jit_solution(5790193779577094986)
XLA Ops:
  7.2 0.7 all-gather.9.cloned.1.call-update
  8.0 0.7 all-gather.11.cloned.1.call-update
  8.7 1.5 copy.33
  10.3 1.5 copy.34
  11.8 1.1 copy.31
  13.1 1.1 copy.32
  14.5 0.6 fusion.42
  15.7 61.9 %all-gather.9.cloned.1.call-done = bf16[4096,128]{1,0:T(8,128)(2,1)} async-done(((bf16[128,128]{1,0:T(8,128)(2,1)}), bf16[4096,128]{1,0:T(8,128)(2,1)}) %all-gather.9.cloned.1.call-update) | async-done | bytes 1048592 | tf_op jit(solution)/shard_map/all_gather | solution.py:115
  77.6 65.1 %all-gather.11.cloned.1.call-done = bf16[4096,128]{1,0:T(8,128)(2,1)} async-done(((bf16[128,128]{1,0:T(8,128)(2,1)}), bf16[4096,128]{1,0:T(8,128)(2,1)}) %all-gather.11.cloned.1.call-update) | async-done | bytes 1048592 | tf_op jit(solution)/shard_map/all_gather | solution.py:117
  142.7 64.0 %all-gather.13.cloned.1.call-done = bf16[4096,128]{0,1:T(8,128)(2,1)} async-done(((bf16[128,128]{0,1:T(8,128)(2,1)}), bf16[4096,128]{0,1:T(8,128)(2,1)}) %all-gather.13.cloned.1.call-update) | async-done | bytes 1048592 | tf_op jit(solution)/shard_map/all_gather | solution.py:116
  206.8 62.7 %all-gather.15.cloned.1.call-done = bf16[4096,128]{0,1:T(8,128)(2,1)} async-done(((bf16[128,128]{0,1:T(8,128)(2,1)}), bf16[4096,128]{0,1:T(8,128)(2,1)}) %all-gather.15.cloned.1.call-update) | async-done | bytes 1048592 | tf_op jit(solution)/shard_map/all_gather | solution.py:118
  269.5 79.9 %while.24 = (s32[]{:T(128)}, f32[128,1,8]{0,2,1:T(8,128)S(1)}, f32[128,1,8]{0,2,1:T(8,128)S(1)}, f32[128,1,8]{0,2,1:T(8,128)S(1)}, f32[128,1,8,128]{0,3,2,1:T(8,...) while((s32[]{:T(128)}, f32[128,1,8]{0,2,1:T(8,128)S(1)}, ...), condition=%wide.region_6.7_spmd.clone, body=%wide.region_1.6_spmd.clone.sunk | while | flops 820517504 | bytes 21996940 | solution.py:79
  269.7 1.3 fusion.71
  271.1 1.4 fusion.69
  272.4 1.9 fusion.72
  274.9 1.6 convolution_bitcast_fusion.4
  276.5 1.6 fusion.74
  278.1 1.3 fusion.75
  279.7 1.3 fusion.71
  281.1 1.4 fusion.69
  282.4 1.9 fusion.72
  284.9 1.6 convolution_bitcast_fusion.4
  286.5 1.6 fusion.74
  288.1 1.3 fusion.75
  289.7 1.3 fusion.71
  291.0 1.4 fusion.69
  292.4 1.9 fusion.72
  294.9 1.6 convolution_bitcast_fusion.4
  296.5 1.6 fusion.74
  298.1 1.3 fusion.75
  299.7 1.3 fusion.71
  301.0 1.4 fusion.69
  302.4 1.9 fusion.72
  304.9 1.6 convolution_bitcast_fusion.4
  306.5 1.6 fusion.74
  308.1 1.3 fusion.75
  309.7 1.3 fusion.71
  311.0 1.4 fusion.69
  312.4 1.9 fusion.72
  314.9 1.6 convolution_bitcast_fusion.4
  316.4 1.6 fusion.74
  318.1 1.3 fusion.75
  319.7 1.3 fusion.71
  321.0 1.4 fusion.69
  322.4 1.9 fusion.72
  324.9 1.6 convolution_bitcast_fusion.4
  326.4 1.6 fusion.74
  328.1 1.3 fusion.75
  329.6 1.3 fusion.71
  331.0 1.4 fusion.69
  332.4 1.9 fusion.72
  334.8 1.6 convolution_bitcast_fusion.4
  336.4 1.6 fusion.74
  338.0 1.3 fusion.75
  339.6 1.3 fusion.71
  341.0 1.4 fusion.69
  342.4 1.9 fusion.72
  344.8 1.6 convolution_bitcast_fusion.4
  346.4 1.6 fusion.74
  348.0 1.3 fusion.75
  349.3 0.8 multiply_reduce_fusion
  350.1 75.8 %psum.7 = f32[]{:T(128)} all-reduce(f32[]{:T(128)} %get-tuple-element.449), channel_id=1, replica_groups=mesh['ctx'=32,'head'=8] {'ctx','head'}, use_global_device_ids=true, to_apply=%region_8.9 | all-reduce | flops 1 | bytes 8 | tf_op jit(solution)/shard_map/psum | solution.py:123
  426.6 0.9 copy.43
  427.4 0.8 copy.42
  (87 shorter events, 6.9 us)
Async XLA Ops:
  7.2 7.3 %copy-start = (s32[32]{0:T(128)S(1)}, s32[32]{0:T(128)}, u32[]{:S(2)}) copy-start(s32[32]{0:T(128)} %param.15) | copy-start | bytes 388
  7.2 70.4 %all-gather.9.cloned.1.call-start = ((), (), s32[]{:S(2)}) async-start(), calls=%async_computation | async-start | bytes 1081344 | tf_op jit(solution)/shard_map/all_gather | solution.py:115
  7.9 134.8 %all-gather.11.cloned.1.call-start = ((), (), s32[]{:S(2)}) async-start(), calls=%async_computation.1 | async-start | bytes 1081344 | tf_op jit(solution)/shard_map/all_gather | solution.py:117
  8.7 198.1 %all-gather.13.cloned.1.call-start = ((), (), s32[]{:S(2)}) async-start(), calls=%async_computation.2 | async-start | bytes 1081344 | tf_op jit(solution)/shard_map/all_gather | solution.py:116
  10.2 259.2 %all-gather.15.cloned.1.call-start = ((), (), s32[]{:S(2)}) async-start(), calls=%async_computation.3 | async-start | bytes 1081344 | tf_op jit(solution)/shard_map/all_gather | solution.py:118
Sparse Core Ops, SparseCore 0:
  9.8 67.7 all-gather.8
  79.4 63.2 all-gather.10
  145.1 61.6 all-gather.12
  209.0 60.4 all-gather.14
where the time goes:
time: 437 us; the launch traced here: 436 us
  waiting for transfers between devices  255 us (58%)
  blocking collectives  75.8 us (17%)
  matrix products  72.6 us (17%)
  between operations  16.3 us (4%)
  other arithmetic  7.76 us (2%)
  local copies, waits for them, and re-layouts  7.28 us (2%)
    psum x1, blocking collectives, shards(): total_squares = lax.psum(square_sum, ('ctx', 'head'))  75.8 us
    all_gather x1, waiting for transfers between devices, shards(): lax.all_gather(dk_three, 'ctx', axis=0, tiled=True)  65.1 us
    all_gather x1, waiting for transfers between devices, shards(): lax.all_gather(v_three, 'ctx', axis=0, tiled=True)  64 us
    all_gather x1, waiting for transfers between devices, shards(): lax.all_gather(dv_three, 'ctx', axis=0, tiled=True)  62.7 us
    all_gather x1, waiting for transfers between devices, shards(): lax.all_gather(k_three, 'ctx', axis=0, tiled=True)  61.9 us
    dot_general x8, matrix products, attend(): jnp.einsum('tghd,sgd->tghs', query_block, ktan_block, preferred_element_t...  15.4 us
    dot_general x8, matrix products, attend(): jnp.einsum('tghs,sgd->tghd', low_weights, value_block, preferred_element_...  13 us
    dot_general x8, matrix products, attend(): jnp.einsum('tghs,sgd->tghd', low_weights, vtan_block, preferred_element_t...  12.5 us
  transfers between devices with their start and end apart: 4, of which 4 were waited for; matrix products, arithmetic and copies ran while one was open for 1% of the time, Pallas kernels for 0%

commit v1 on v0

--- a/solution.py
+++ b/solution.py
@@ -120,7 +120,7 @@
         jnp.int32(0),
     )
     attended, probe_out, square_sum = finish(final, width)
-    total_squares = lax.psum(square_sum, ("ctx", "head"))
+    total_squares = jnp.sum(lax.all_gather(square_sum, ("ctx", "head")), axis=0)
     entries = row_count * width * count * lax.axis_size("head")
     probe_norm = jnp.sqrt(total_squares / entries)
     return (attended, probe_out, probe_norm)

time: 437 us -> 445 us (1.018)
  matrix products: 72.6 us -> 79.8 us
    psum x1 -> x0, blocking collectives: 75.8 us -> none  [shards(): total_squares = lax.psum(square_sum, ('ctx', 'head'))]
    unnamed x0 -> x1, blocking collectives: none -> 75.5 us
    dot_general x8, matrix products: 13 us -> 20.4 us  [attend(): jnp.einsum('tghs,sgd->tghd', low_weights, value_block, preferred_element_...]
where the time goes in v1:
time: 445 us; the launch traced here: 444 us
  waiting for transfers between devices  254 us (57%)
  matrix products  79.8 us (18%)
  blocking collectives  75.5 us (17%)
  between operations  16.3 us (4%)
  other arithmetic  9.38 us (2%)
  local copies, waits for them, and re-layouts  8.04 us (2%)
    unnamed x1, blocking collectives  75.5 us
    all_gather x1, waiting for transfers between devices, shards(): lax.all_gather(dk_three, 'ctx', axis=0, tiled=True)  65 us
    all_gather x1, waiting for transfers between devices, shards(): lax.all_gather(k_three, 'ctx', axis=0, tiled=True)  64 us
    all_gather x1, waiting for transfers between devices, shards(): lax.all_gather(dv_three, 'ctx', axis=0, tiled=True)  62.8 us
    all_gather x1, waiting for transfers between devices, shards(): lax.all_gather(v_three, 'ctx', axis=0, tiled=True)  61 us
    dot_general x8, matrix products, attend(): jnp.einsum('tghs,sgd->tghd', low_weights, value_block, preferred_element_...  20.4 us
    dot_general x8, matrix products, attend(): jnp.einsum('tghd,sgd->tghs', query_block, ktan_block, preferred_element_t...  15.2 us
    dot_general x8, matrix products, attend(): jnp.einsum('tghs,sgd->tghd', low_weights, vtan_block, preferred_element_t...  12.5 us
  transfers between devices with their start and end apart: 4, of which 4 were waited for; matrix products, arithmetic and copies ran while one was open for 1% of the time, Pallas kernels for 0%

profile of v1, /device:TPU:1, one launch (start us, length us, event | category | flops | bytes accessed | tf_op | source)
XLA Modules:
  0.0 444.0 jit_solution(7224180549734315628)
XLA Ops:
  7.2 1.5 copy.33
  8.8 1.5 copy.34
  10.3 0.7 all-gather.9.cloned.1.call-update
  11.6 1.1 copy.31
  13.0 1.1 copy.32
  14.3 0.6 fusion.42
  15.4 61.0 %all-gather.13.cloned.1.call-done = bf16[4096,128]{0,1:T(8,128)(2,1)} async-done(((bf16[128,128]{0,1:T(8,128)(2,1)}), bf16[4096,128]{0,1:T(8,128)(2,1)}) %all-gather.13.cloned.1.call-update) | async-done | bytes 1048592 | tf_op jit(solution)/shard_map/all_gather | solution.py:116
  76.5 62.8 %all-gather.15.cloned.1.call-done = bf16[4096,128]{0,1:T(8,128)(2,1)} async-done(((bf16[128,128]{0,1:T(8,128)(2,1)}), bf16[4096,128]{0,1:T(8,128)(2,1)}) %all-gather.15.cloned.1.call-update) | async-done | bytes 1048592 | tf_op jit(solution)/shard_map/all_gather | solution.py:118
  139.3 64.0 %all-gather.9.cloned.1.call-done = bf16[4096,128]{1,0:T(8,128)(2,1)} async-done(((bf16[128,128]{1,0:T(8,128)(2,1)}), bf16[4096,128]{1,0:T(8,128)(2,1)}) %all-gather.9.cloned.1.call-update) | async-done | bytes 1048592 | tf_op jit(solution)/shard_map/all_gather | solution.py:115
  203.3 65.0 %all-gather.11.cloned.1.call-done = bf16[4096,128]{1,0:T(8,128)(2,1)} async-done(((bf16[128,128]{1,0:T(8,128)(2,1)}), bf16[4096,128]{1,0:T(8,128)(2,1)}) %all-gather.11.cloned.1.call-update) | async-done | bytes 1048592 | tf_op jit(solution)/shard_map/all_gather | solution.py:117
  268.3 86.9 %while.24 = (s32[]{:T(128)}, f32[128,1,8]{0,2,1:T(8,128)S(1)}, f32[128,1,8]{0,2,1:T(8,128)S(1)}, f32[128,1,8]{0,2,1:T(8,128)S(1)}, f32[128,1,8,128]{0,3,2,1:T(8,...) while((s32[]{:T(128)}, f32[128,1,8]{0,2,1:T(8,128)S(1)}, ...), condition=%wide.region_6.7_spmd.clone, body=%wide.region_1.6_spmd.clone.sunk | while | flops 820517504 | bytes 21996932 | solution.py:79
  268.5 1.4 fusion.69
  269.9 1.3 fusion.71
  271.3 1.9 fusion.72
  273.2 1.6 convolution_bitcast_fusion.4
  274.7 1.3 fusion.75
  276.0 2.4 fusion.74
  279.2 1.4 fusion.69
  280.6 1.3 fusion.71
  281.9 1.9 fusion.72
  283.9 1.6 convolution_bitcast_fusion.4
  285.4 1.3 fusion.75
  286.7 2.6 fusion.74
  290.1 1.4 fusion.69
  291.5 1.3 fusion.71
  292.8 1.9 fusion.72
  294.7 1.6 convolution_bitcast_fusion.4
  296.3 1.3 fusion.75
  297.6 2.6 fusion.74
  301.0 1.4 fusion.69
  302.4 1.3 fusion.71
  303.7 1.9 fusion.72
  305.6 1.6 convolution_bitcast_fusion.4
  307.2 1.3 fusion.75
  308.5 2.6 fusion.74
  311.9 1.4 fusion.69
  313.3 1.3 fusion.71
  314.6 1.9 fusion.72
  316.5 1.6 convolution_bitcast_fusion.4
  318.1 1.3 fusion.75
  319.4 2.6 fusion.74
  322.8 1.4 fusion.69
  324.2 1.3 fusion.71
  325.5 1.9 fusion.72
  327.4 1.6 convolution_bitcast_fusion.4
  329.0 1.3 fusion.75
  330.3 2.6 fusion.74
  333.7 1.4 fusion.69
  335.1 1.3 fusion.71
  336.4 1.9 fusion.72
  338.3 1.6 convolution_bitcast_fusion.4
  339.9 1.3 fusion.75
  341.2 2.6 fusion.74
  344.6 1.4 fusion.69
  346.0 1.3 fusion.71
  347.3 1.9 fusion.72
  349.2 1.6 convolution_bitcast_fusion.4
  350.8 1.3 fusion.75
  352.1 2.6 fusion.74
  355.2 1.8 multiply_reduce_fusion
  357.1 0.8 dynamic-update-slice
  357.8 75.5 %all-reduce = f32[256]{0:T(256)S(1)} all-reduce(f32[256]{0:T(256)S(1)} %dynamic-update-slice), channel_id=1, replica_groups=mesh['ctx'=32,'head'=8] {'ctx','head'}, use_global_device_ids=true, to_apply=%add | all-reduce | flops 256 | bytes 2048
  434.6 0.9 copy.42
  435.5 0.9 copy.43
  (90 shorter events, 8.0 us)
Async XLA Ops:
  7.2 7.1 %copy-start = (s32[32]{0:T(128)S(1)}, s32[32]{0:T(128)}, u32[]{:S(2)}) copy-start(s32[32]{0:T(128)} %param.15) | copy-start | bytes 388
  7.2 69.3 %all-gather.13.cloned.1.call-start = ((), (), s32[]{:S(2)}) async-start(), calls=%async_computation.2 | async-start | bytes 1081344 | tf_op jit(solution)/shard_map/all_gather | solution.py:116
  8.7 130.6 %all-gather.15.cloned.1.call-start = ((), (), s32[]{:S(2)}) async-start(), calls=%async_computation.3 | async-start | bytes 1081344 | tf_op jit(solution)/shard_map/all_gather | solution.py:118
  10.3 193.0 %all-gather.9.cloned.1.call-start = ((), (), s32[]{:S(2)}) async-start(), calls=%async_computation | async-start | bytes 1081344 | tf_op jit(solution)/shard_map/all_gather | solution.py:115
  11.0 257.3 %all-gather.11.cloned.1.call-start = ((), (), s32[]{:S(2)}) async-start(), calls=%async_computation.1 | async-start | bytes 1081344 | tf_op jit(solution)/shard_map/all_gather | solution.py:117
Sparse Core Ops, SparseCore 0:
  10.3 66.0 all-gather.12
  78.8 60.4 all-gather.14
  141.1 62.0 all-gather.8
  205.0 63.2 all-gather.10

commit v2 on v0

--- a/solution.py
+++ b/solution.py
@@ -120,7 +120,7 @@
         jnp.int32(0),
     )
     attended, probe_out, square_sum = finish(final, width)
-    total_squares = lax.psum(square_sum, ("ctx", "head"))
+    total_squares = lax.psum(lax.psum(square_sum, "head"), "ctx")
     entries = row_count * width * count * lax.axis_size("head")
     probe_norm = jnp.sqrt(total_squares / entries)
     return (attended, probe_out, probe_norm)

time: 437 us -> 439 us (level)
    psum x1 -> x2, blocking collectives: 75.8 us -> 78 us  [shards(): total_squares = lax.psum(lax.psum(square_sum, 'head'), 'ctx')]
where the time goes in v2:
time: 439 us; the launch traced here: 438 us
  waiting for transfers between devices  255 us (58%)
  blocking collectives  78 us (18%)
  matrix products  72.6 us (17%)
  between operations  16.3 us (4%)
  other arithmetic  7.76 us (2%)
  local copies, waits for them, and re-layouts  7.28 us (2%)
    psum x2, blocking collectives, shards(): total_squares = lax.psum(lax.psum(square_sum, 'head'), 'ctx')  78 us
    all_gather x1, waiting for transfers between devices, shards(): lax.all_gather(dk_three, 'ctx', axis=0, tiled=True)  65.1 us
    all_gather x1, waiting for transfers between devices, shards(): lax.all_gather(v_three, 'ctx', axis=0, tiled=True)  64 us
    all_gather x1, waiting for transfers between devices, shards(): lax.all_gather(dv_three, 'ctx', axis=0, tiled=True)  62.7 us
    all_gather x1, waiting for transfers between devices, shards(): lax.all_gather(k_three, 'ctx', axis=0, tiled=True)  61.9 us
    dot_general x8, matrix products, attend(): jnp.einsum('tghd,sgd->tghs', query_block, ktan_block, preferred_element_t...  15.4 us
    dot_general x8, matrix products, attend(): jnp.einsum('tghs,sgd->tghd', low_weights, value_block, preferred_element_...  13 us
    dot_general x8, matrix products, attend(): jnp.einsum('tghs,sgd->tghd', low_weights, vtan_block, preferred_element_t...  12.5 us
  transfers between devices with their start and end apart: 4, of which 4 were waited for; matrix products, arithmetic and copies ran while one was open for 1% of the time, Pallas kernels for 0%

profile of v2, /device:TPU:1, one launch (start us, length us, event | category | flops | bytes accessed | tf_op | source)
XLA Modules:
  0.0 438.2 jit_solution(3702050877883943730)
XLA Ops:
  7.2 0.7 all-gather.9.cloned.1.call-update
  8.0 0.7 all-gather.11.cloned.1.call-update
  8.7 1.5 copy.33
  10.3 1.5 copy.34
  11.8 1.1 copy.31
  13.1 1.1 copy.32
  15.7 61.9 %all-gather.9.cloned.1.call-done = bf16[4096,128]{1,0:T(8,128)(2,1)} async-done(((bf16[128,128]{1,0:T(8,128)(2,1)}), bf16[4096,128]{1,0:T(8,128)(2,1)}) %all-gather.9.cloned.1.call-update) | async-done | bytes 1048592 | tf_op jit(solution)/shard_map/all_gather | solution.py:115
  77.6 65.1 %all-gather.11.cloned.1.call-done = bf16[4096,128]{1,0:T(8,128)(2,1)} async-done(((bf16[128,128]{1,0:T(8,128)(2,1)}), bf16[4096,128]{1,0:T(8,128)(2,1)}) %all-gather.11.cloned.1.call-update) | async-done | bytes 1048592 | tf_op jit(solution)/shard_map/all_gather | solution.py:117
  142.7 64.0 %all-gather.13.cloned.1.call-done = bf16[4096,128]{0,1:T(8,128)(2,1)} async-done(((bf16[128,128]{0,1:T(8,128)(2,1)}), bf16[4096,128]{0,1:T(8,128)(2,1)}) %all-gather.13.cloned.1.call-update) | async-done | bytes 1048592 | tf_op jit(solution)/shard_map/all_gather | solution.py:116
  206.8 62.7 %all-gather.15.cloned.1.call-done = bf16[4096,128]{0,1:T(8,128)(2,1)} async-done(((bf16[128,128]{0,1:T(8,128)(2,1)}), bf16[4096,128]{0,1:T(8,128)(2,1)}) %all-gather.15.cloned.1.call-update) | async-done | bytes 1048592 | tf_op jit(solution)/shard_map/all_gather | solution.py:118
  269.5 79.9 %while.24 = (s32[]{:T(128)}, f32[128,1,8]{0,2,1:T(8,128)S(1)}, f32[128,1,8]{0,2,1:T(8,128)S(1)}, f32[128,1,8]{0,2,1:T(8,128)S(1)}, f32[128,1,8,128]{0,3,2,1:T(8,...) while((s32[]{:T(128)}, f32[128,1,8]{0,2,1:T(8,128)S(1)}, ...), condition=%wide.region_6.7_spmd.clone, body=%wide.region_1.6_spmd.clone.sunk | while | flops 820517504 | bytes 21996940 | solution.py:79
  269.7 1.3 fusion.71
  271.1 1.4 fusion.69
  272.4 1.9 fusion.72
  274.9 1.6 convolution_bitcast_fusion.4
  276.5 1.6 fusion.74
  278.1 1.3 fusion.75
  279.7 1.3 fusion.71
  281.1 1.4 fusion.69
  282.4 1.9 fusion.72
  284.9 1.6 convolution_bitcast_fusion.4
  286.5 1.6 fusion.74
  288.1 1.3 fusion.75
  289.7 1.3 fusion.71
  291.0 1.4 fusion.69
  292.4 1.9 fusion.72
  294.9 1.6 convolution_bitcast_fusion.4
  296.5 1.6 fusion.74
  298.1 1.3 fusion.75
  299.7 1.3 fusion.71
  301.0 1.4 fusion.69
  302.4 1.9 fusion.72
  304.9 1.6 convolution_bitcast_fusion.4
  306.5 1.6 fusion.74
  308.1 1.3 fusion.75
  309.7 1.3 fusion.71
  311.0 1.4 fusion.69
  312.4 1.9 fusion.72
  314.9 1.6 convolution_bitcast_fusion.4
  316.4 1.6 fusion.74
  318.1 1.3 fusion.75
  319.7 1.3 fusion.71
  321.0 1.4 fusion.69
  322.4 1.9 fusion.72
  324.9 1.6 convolution_bitcast_fusion.4
  326.4 1.6 fusion.74
  328.1 1.3 fusion.75
  329.6 1.3 fusion.71
  331.0 1.4 fusion.69
  332.4 1.9 fusion.72
  334.8 1.6 convolution_bitcast_fusion.4
  336.4 1.6 fusion.74
  338.0 1.3 fusion.75
  339.6 1.3 fusion.71
  341.0 1.4 fusion.69
  342.4 1.9 fusion.72
  344.8 1.6 convolution_bitcast_fusion.4
  346.4 1.6 fusion.74
  348.0 1.3 fusion.75
  349.3 0.8 multiply_reduce_fusion
  350.1 20.9 %psum.14 = f32[]{:T(128)} all-reduce(f32[]{:T(128)} %get-tuple-element.449), channel_id=1, replica_groups=mesh['ctx'=32,'head'=8] {'head'}, use_global_device_ids=true, to_apply=%region_8.9 | all-reduce | flops 1 | bytes 8 | tf_op jit(solution)/shard_map/psum | solution.py:123
  371.0 57.1 %psum.15 = f32[]{:T(128)} all-reduce(f32[]{:T(128)} %psum.14), channel_id=1, replica_groups=mesh['ctx'=32,'head'=8] {'ctx'}, use_global_device_ids=true, to_apply=%region_9.10 | all-reduce | flops 1 | bytes 8 | tf_op jit(solution)/shard_map/psum | solution.py:123
  428.8 0.9 copy.43
  429.7 0.8 copy.42
  (88 shorter events, 7.6 us)
Async XLA Ops:
  7.2 7.3 %copy-start = (s32[32]{0:T(128)S(1)}, s32[32]{0:T(128)}, u32[]{:S(2)}) copy-start(s32[32]{0:T(128)} %param.15) | copy-start | bytes 388
  7.2 70.4 %all-gather.9.cloned.1.call-start = ((), (), s32[]{:S(2)}) async-start(), calls=%async_computation | async-start | bytes 1081344 | tf_op jit(solution)/shard_map/all_gather | solution.py:115
  7.9 134.8 %all-gather.11.cloned.1.call-start = ((), (), s32[]{:S(2)}) async-start(), calls=%async_computation.1 | async-start | bytes 1081344 | tf_op jit(solution)/shard_map/all_gather | solution.py:117
  8.7 198.1 %all-gather.13.cloned.1.call-start = ((), (), s32[]{:S(2)}) async-start(), calls=%async_computation.2 | async-start | bytes 1081344 | tf_op jit(solution)/shard_map/all_gather | solution.py:116
  10.2 259.2 %all-gather.15.cloned.1.call-start = ((), (), s32[]{:S(2)}) async-start(), calls=%async_computation.3 | async-start | bytes 1081344 | tf_op jit(solution)/shard_map/all_gather | solution.py:118
Sparse Core Ops, SparseCore 0:
  9.8 67.7 all-gather.8
  79.4 63.2 all-gather.10
  145.1 61.6 all-gather.12
  209.0 60.4 all-gather.14
